TPU v7x, 256 devices: a whole 4x4x8 slice. The times are simulated.
256 devices in a mesh: cols: 32 (over y, z), mem: 8 (over x, core).
Axes of the slice: x: 4, y: 4, z: 8, core: 2. Of those that a mesh axis runs over, the one named last changes fastest.
Arguments:
- state: float32 [80, 1048576], P('mem', 'cols'), may hold values from -6 to 6
- obs_value: float32 [4, 1024], P(None, 'cols'), may hold values from -6 to 6
- obs_var: float32 [4, 1024], P(None, 'cols'), may hold values from 0.2 to 2
- owner: int32 [4, 1024, 1], P(None, 'cols'), may hold values from 0 to 31; in each aligned block of 32 rows (0 to 31, 32 to 63, ..., all dimensions but the last counted through in order) at most 2 rows name the same one
- tile_of: int32 [4, 1024], P(None, 'cols'), may hold values from 0 to 63
- offsets: int32 [4, 1024, 4], P(None, 'cols'), may hold values from 0 to 511
- accept: int32 [4, 1024], P(None, 'cols'), may hold values 0 or 1
- loc_mask: int32 [2048, 4, 8], P(('cols', 'mem')), may hold values 0 or 1
Outputs:
- posterior: float32 [80, 1048576], P(None, ('cols', 'mem'))
Inputs may be any that keep to these rules, and one draw needn't show every extreme that they name: Within the 32 observations of one batch held by one index of cols, no owner is named more than 2 times, and that many is reached.
All inputs are finite; a program needn't handle non-finite values. No bound on the sum of `accept` or of `loc_mask` on one device may be relied on, other than what follows from the above.
Results may differ from a plain program's by a relative error of at most 0.0002.
Values sent between devices are 32-bit elements; how exact they have to be, the bound alone decides.
A program may use at most 64 MiB of HBM per device.

v0:
```python
import jax
import jax.numpy as jnp
from jax import lax
from jax.sharding import PartitionSpec as P

epsilon = 1e-05
EXACT = lax.Precision.HIGHEST


def innovations(prior_obs, observed, obs_noise, accepted):
    members = prior_obs.shape[0]
    mean_prior = jnp.mean(prior_obs, axis=0)
    spread = prior_obs - mean_prior
    spread_var = jnp.sum(spread * spread, axis=0) / (members - 1) + epsilon
    denominator = spread_var + obs_noise
    mean_shift = spread_var / denominator * (observed - mean_prior)
    factor = jnp.sqrt(obs_noise / denominator) - 1.0
    increment = accepted * (mean_shift + factor * spread)
    scaled = spread / ((members - 1) * spread_var)
    return (increment, scaled)


def local(state, obs_value, obs_var, owner, tile_of, offsets, accept, loc_mask):
    col_devices = lax.axis_size("cols")
    mem_devices = lax.axis_size("mem")
    source = lax.axis_index("cols")
    mem_index = lax.axis_index("mem")
    batch_total, per_src = obs_value.shape
    pick_count = offsets.shape[2]
    members = state.shape[0] * mem_devices
    cell_count = state.shape[1] // mem_devices
    tiles_here = loc_mask.shape[0]
    tile_len = cell_count // tiles_here
    block_count = loc_mask.shape[2]
    batch_obs = per_src * col_devices
    block_len = batch_obs // block_count
    capacity = max(2, 2 * per_src // col_devices)
    slot_count = col_devices * capacity
    destination = owner[:, :, 0]
    ordinal = jnp.arange(per_src, dtype=jnp.int32)
    same_owner = destination[:, :, None] == destination[:, None, :]
    earlier = (ordinal[None, :] < ordinal[:, None])[None]
    slot_rank = jnp.sum((same_owner & earlier).astype(jnp.int32), axis=2)
    batch_rows = jnp.broadcast_to(
        jnp.arange(batch_total, dtype=jnp.int32)[:, None], destination.shape
    )
    position = jnp.broadcast_to(source * per_src + ordinal, destination.shape)
    fields = jnp.concatenate(
        [tile_of[:, :, None], accept[:, :, None], position[:, :, None], offsets], axis=2
    )
    blank_int = (
        jnp.zeros((batch_total, col_devices, capacity, 3 + pick_count), jnp.int32)
        .at[:, :, :, 2]
        .set(-1)
    )
    sent_int = blank_int.at[batch_rows, destination, slot_rank].set(fields)
    blank_val = (
        jnp.zeros((batch_total, col_devices, capacity, 2), jnp.float32).at[:, :, :, 1].set(1.0)
    )
    sent_val = blank_val.at[batch_rows, destination, slot_rank].set(
        jnp.stack([obs_value, obs_var], axis=2)
    )
    arrived_int = lax.all_to_all(sent_int, "cols", split_axis=1, concat_axis=1, tiled=True).reshape(
        batch_total, slot_count, 3 + pick_count
    )
    arrived_val = lax.all_to_all(sent_val, "cols", split_axis=1, concat_axis=1, tiled=True).reshape(
        batch_total, slot_count, 2
    )
    obs_tile = arrived_int[:, :, 0]
    obs_flag = arrived_int[:, :, 1].astype(jnp.float32)
    obs_pos = arrived_int[:, :, 2]
    obs_off = arrived_int[:, :, 3:]
    observed = arrived_val[:, :, 0]
    obs_noise = arrived_val[:, :, 1]
    targets = jnp.where(obs_pos >= 0, obs_pos, batch_obs)
    ensemble = lax.all_to_all(state, "mem", split_axis=1, concat_axis=0, tiled=True)
    for batch_no in range(batch_total):
        local_cell = (
            obs_tile[batch_no][:, None] * tile_len + obs_off[batch_no] - mem_index * cell_count
        )
        inside = (local_cell >= 0) & (local_cell < cell_count) & (obs_pos[batch_no] >= 0)[:, None]
        flat_cells = jnp.clip(local_cell, 0, cell_count - 1).reshape(-1)
        picked = jnp.take(ensemble, flat_cells, axis=1).reshape(members, slot_count, pick_count)
        prior_obs = lax.psum(
            jnp.sum(jnp.where(inside[None], picked, 0.0), axis=2) / pick_count, "mem"
        )
        increment, scaled = innovations(
            prior_obs, observed[batch_no], obs_noise[batch_no], obs_flag[batch_no]
        )
        blank_panel = jnp.zeros((members, batch_obs), jnp.float32)
        placed_inc = blank_panel.at[:, targets[batch_no]].add(increment, mode="drop")
        placed_scl = blank_panel.at[:, targets[batch_no]].add(scaled, mode="drop")
        inc_all, scl_all = lax.psum((placed_inc, placed_scl), "cols")
        mask_now = loc_mask[:, batch_no, :].astype(jnp.float32)
        mean_state = jnp.mean(ensemble, axis=0)
        deviation = (ensemble - mean_state).reshape(members, tiles_here, tile_len)
        per_block = jnp.einsum(
            "nbk,mbk->bnm",
            scl_all.reshape(members, block_count, block_len),
            inc_all.reshape(members, block_count, block_len),
            precision=EXACT,
        )
        mixing = jnp.einsum("tb,bnm->tnm", mask_now, per_block, precision=EXACT)
        change = jnp.einsum("tnm,nti->mti", mixing, deviation, precision=EXACT).reshape(
            members, cell_count
        )
        ensemble = ensemble + change
    return ensemble


def solution(mesh):
    return jax.shard_map(
        local,
        mesh=mesh,
        in_specs=(
            P("mem", "cols"),
            P(None, "cols"),
            P(None, "cols"),
            P(None, "cols", None),
            P(None, "cols"),
            P(None, "cols", None),
            P(None, "cols"),
            P(("cols", "mem"), None, None),
        ),
        out_specs=P(None, ("cols", "mem")),
        check_vma=False,
    )
```

profile of v0, /device:TPU:2, one launch (start us, length us, event | category | flops | bytes accessed | tf_op | source)
XLA Modules:
  0.0 843.9 jit_solution(13650649832202001526)
XLA Ops:
  10.0 7.9 scatter_fusion.1
  19.1 11.5 %all-to-all-start.2 = ((f32[4,32,2,2]{0,3,2,1:T(2,128)}), f32[4,32,2,2]{0,3,2,1:T(2,128)S(1)}, u32[]{:S(2)}, u32[]{:S(2)}) async-start(f32[4,32,2,2]{0,3,2,1:T(2,128)} %copy.270), calls=%async_computation.2 | async-start | bytes 131072 | tf_op jit(solution)/shard_map/all_to_all | solution.py:66
  31.4 7.9 scatter_fusion
  40.0 1.2 copy.348
  41.3 2.2 copy.253
  43.5 9.8 %all-to-all-start.1 = ((s32[4,32,2,7]{3,2,0,1:T(2,128)}), s32[4,32,2,7]{3,2,0,1:T(2,128)S(1)}, u32[]{:S(2)}, u32[]{:S(2)}) async-start(s32[4,32,2,7]{3,2,0,1:T(2,128)} %copy.261), calls=%async_computation.1 | async-start | bytes 262144 | tf_op jit(solution)/shard_map/all_to_all | solution.py:63
  54.2 9.5 %all-to-all-done.1 = s32[4,32,2,7]{3,2,0,1:T(2,128)S(1)} async-done(((s32[4,32,2,7]{3,2,0,1:T(2,128)}), s32[4,32,2,7]{3,2,0,1:T(2,128)S(1)}, u32[]{:S(2)}, u32[]{:S(2)}) %all-to-all-start.1) | async-done | bytes 7200 | tf_op jit(solution)/shard_map/all_to_all | solution.py:63
  63.7 4.8 all-to-all-start
  75.7 18.6 %all-to-all-done = f32[10,8,4096]{2,0,1:T(8,128)S(1)} async-done(((f32[10,8,4096]{2,0,1:T(8,128)}), f32[10,8,4096]{2,0,1:T(8,128)S(1)}, u32[]{:S(2)}, u32[]{:S(2)}) %all-to-all-start) | async-done | bytes 1310752 | tf_op jit(solution)/shard_map/all_to_all | solution.py:76
  94.5 1.8 copy.266
  96.3 2.4 gather_fusion
  99.8 21.7 %psum.84 = f32[80,64]{0,1:T(8,128)S(1)} all-reduce(f32[80,64]{0,1:T(8,128)S(1)} %broadcast_multiply_fusion.3), channel_id=1, replica_groups=mesh['cols'=32,'mem'=8] {'mem'}, use_global_device_ids=true, to_apply=%region_4.6 | all-reduce | flops 5120 | bytes 40960 | tf_op jit(solution)/shard_map/psum | solution.py:84
  122.5 1.2 scatter_custom_fusion.3
  131.7 1.3 broadcast_subtract_fusion
  133.0 139.0 %all-reduce.15.cloned.1.call-done = (f32[80,8,128]{2,0,1:T(8,128)}, f32[80,8,128]{2,0,1:T(8,128)}) async-done(((f32[80,8,128]{2,0,1:T(8,128)}, f32[80,8,128]{2,0,1:T(8,128)}), (f32[80,8,128]{2,0,1:T(8,128)}, f32[80,8,128]{2,0,1:T(8,128)})) %all-reduce.15.cloned.1.call-update) | async-done | bytes 655376 | tf_op jit(solution)/shard_map/psum | solution.py:93
  272.0 1.8 fusion.125
  274.4 2.1 fusion
  276.6 1.2 copy-done.4
  277.8 1.2 add.373
  279.0 2.8 copy.284
  281.8 2.4 gather_fusion.1
  285.3 20.7 %psum.87 = f32[80,64]{0,1:T(8,128)S(1)} all-reduce(f32[80,64]{0,1:T(8,128)S(1)} %broadcast_multiply_fusion.2), channel_id=1, replica_groups=mesh['cols'=32,'mem'=8] {'mem'}, use_global_device_ids=true, to_apply=%region_14.16 | all-reduce | flops 5120 | bytes 40960 | tf_op jit(solution)/shard_map/psum | solution.py:84
  307.0 1.8 scatter_custom_fusion.5
  308.8 2.0 copy.288
  310.7 1.8 scatter_custom_fusion.4
  312.5 2.0 copy.286
  316.7 1.8 copy.278
  318.5 2.7 reshape.653
  321.2 1.9 add_reduce_fusion
  323.1 138.9 %all-reduce.13.cloned.1.call-done = (f32[80,8,128]{2,0,1:T(8,128)}, f32[80,8,128]{2,0,1:T(8,128)}) async-done(((f32[80,8,128]{2,0,1:T(8,128)}, f32[80,8,128]{2,0,1:T(8,128)}), (f32[80,8,128]{2,0,1:T(8,128)}, f32[80,8,128]{2,0,1:T(8,128)})) %all-reduce.13.cloned.1.call-update) | async-done | bytes 655376 | tf_op jit(solution)/shard_map/psum | solution.py:93
  462.1 1.7 fusion.126
  464.3 3.9 fusion.122
  468.3 1.2 copy-done.5
  473.2 20.7 %psum.90 = f32[80,64]{0,1:T(8,128)S(1)} all-reduce(f32[80,64]{0,1:T(8,128)S(1)} %broadcast_multiply_fusion.1), channel_id=1, replica_groups=mesh['cols'=32,'mem'=8] {'mem'}, use_global_device_ids=true, to_apply=%region_23.25 | all-reduce | flops 5120 | bytes 40960 | tf_op jit(solution)/shard_map/psum | solution.py:84
  499.3 147.3 %all-reduce.11.cloned.1.call-done = (f32[80,8,128]{2,0,1:T(8,128)}, f32[80,8,128]{2,0,1:T(8,128)}) async-done(((f32[80,8,128]{2,0,1:T(8,128)}, f32[80,8,128]{2,0,1:T(8,128)}), (f32[80,8,128]{2,0,1:T(8,128)}, f32[80,8,128]{2,0,1:T(8,128)})) %all-reduce.11.cloned.1.call-update) | async-done | bytes 655376 | tf_op jit(solution)/shard_map/psum | solution.py:93
  646.6 1.7 fusion.127
  648.8 1.4 fusion.10
  650.4 1.2 copy-done.7
  651.5 1.2 add.398
  652.8 2.8 copy.308
  655.6 2.3 gather_fusion.3
  658.2 20.7 %psum.93 = f32[80,64]{0,1:T(8,128)S(1)} all-reduce(f32[80,64]{0,1:T(8,128)S(1)} %broadcast_multiply_fusion), channel_id=1, replica_groups=mesh['cols'=32,'mem'=8] {'mem'}, use_global_device_ids=true, to_apply=%region_32.34 | all-reduce | flops 5120 | bytes 40960 | tf_op jit(solution)/shard_map/psum | solution.py:84
  679.2 1.4 scatter_custom_fusion.9
  683.7 147.6 %all-reduce.9.cloned.1.call-done = (f32[80,8,128]{2,0,1:T(8,128)}, f32[80,8,128]{2,0,1:T(8,128)}) async-done(((f32[80,8,128]{2,0,1:T(8,128)}, f32[80,8,128]{2,0,1:T(8,128)}), (f32[80,8,128]{2,0,1:T(8,128)}, f32[80,8,128]{2,0,1:T(8,128)})) %all-reduce.9.cloned.1.call-update) | async-done | bytes 655376 | tf_op jit(solution)/shard_map/psum | solution.py:93
  831.2 1.7 fusion.128
  833.5 1.4 convolution_bitcast_fusion
  835.0 1.2 copy-done.8
  836.2 1.2 add.410
  (200 shorter events, 43.2 us)
Async XLA Ops:
  6.5 24.8 %copy-start.10 = (s32[4,32,2,7]{3,2,1,0:T(2,128)S(1)}, s32[4,32,2,7]{3,2,1,0:T(2,128)}, u32[]{:S(2)}) copy-start(s32[4,32,2,7]{3,2,1,0:T(2,128)} %constant.122.clone.1) | copy-start | bytes 21508
  6.5 24.1 %copy-start.18 = (s32[8,4,8]{2,1,0:T(4,128)S(1)}, s32[8,4,8]{2,1,0:T(4,128)}, u32[]{:S(2)}) copy-start(s32[8,4,8]{2,1,0:T(4,128)} %param.21) | copy-start | bytes 3076
  6.5 24.7 %copy-start.40 = (s32[4,32]{1,0:T(4,128)S(1)}, s32[4,32]{1,0:T(4,128)}, u32[]{:S(2)}) copy-start(s32[4,32]{1,0:T(4,128)} %param.20) | copy-start | bytes 1540
  6.5 24.7 %copy-start.21 = (s32[4,32,4]{1,2,0:T(4,128)S(1)}, s32[4,32,4]{1,2,0:T(4,128)}, u32[]{:S(2)}) copy-start(s32[4,32,4]{1,2,0:T(4,128)} %param.19) | copy-start | bytes 6148
  6.5 24.7 %copy-start.41 = (s32[4,32]{1,0:T(4,128)S(1)}, s32[4,32]{1,0:T(4,128)}, u32[]{:S(2)}) copy-start(s32[4,32]{1,0:T(4,128)} %param.18) | copy-start | bytes 1540
  18.0 22.0 %copy-start.11 = (f32[10,32768]{1,0:T(8,128)S(1)}, f32[10,32768]{1,0:T(8,128)}, u32[]{:S(2)}) copy-start(f32[10,32768]{1,0:T(8,128)} %param.14) | copy-start | bytes 3932164
  19.1 24.4 %all-to-all-start.2 = ((f32[4,32,2,2]{0,3,2,1:T(2,128)}), f32[4,32,2,2]{0,3,2,1:T(2,128)S(1)}, u32[]{:S(2)}, u32[]{:S(2)}) async-start(f32[4,32,2,2]{0,3,2,1:T(2,128)} %copy.270), calls=%async_computation.2 | async-start | bytes 131072 | tf_op jit(solution)/shard_map/all_to_all | solution.py:66
  43.5 20.2 %all-to-all-start.1 = ((s32[4,32,2,7]{3,2,0,1:T(2,128)}), s32[4,32,2,7]{3,2,0,1:T(2,128)S(1)}, u32[]{:S(2)}, u32[]{:S(2)}) async-start(s32[4,32,2,7]{3,2,0,1:T(2,128)} %copy.261), calls=%async_computation.1 | async-start | bytes 262144 | tf_op jit(solution)/shard_map/all_to_all | solution.py:63
  63.7 30.5 %all-to-all-start = ((f32[10,8,4096]{2,0,1:T(8,128)}), f32[10,8,4096]{2,0,1:T(8,128)S(1)}, u32[]{:S(2)}, u32[]{:S(2)}) async-start(f32[10,8,4096]{2,0,1:T(8,128)} %copy.253), calls=%async_computation | async-start | bytes 4194304 | tf_op jit(solution)/shard_map/all_to_all | solution.py:76
  68.6 203.5 %all-reduce.15.cloned.1.call-start = ((), (), s32[]{:S(2)}) async-start(), calls=%async_computation.6 | async-start | bytes 1310720 | tf_op jit(solution)/shard_map/psum | solution.py:93
  70.2 24.1 %copy-start.12 = (s32[1,64,4]{2,1,0:T(8,128)}, s32[1,64,4]{2,1,0:T(8,128)S(1)}, u32[]{:S(2)}) copy-start(s32[1,64,4]{2,1,0:T(8,128)S(1)} %get-tuple-element.71) | copy-start | bytes 3076
  70.2 24.1 %copy-start.14 = (s32[1,64,4]{2,1,0:T(8,128)}, s32[1,64,4]{2,1,0:T(8,128)S(1)}, u32[]{:S(2)}) copy-start(s32[1,64,4]{2,1,0:T(8,128)S(1)} %get-tuple-element.68) | copy-start | bytes 3076
  94.5 1.9 copy-start.3
  123.7 3.3 copy-start.19
  123.7 3.3 copy-start.20
  123.7 3.3 copy-start.22
  123.7 3.3 copy-start.23
  123.7 3.3 copy-start.35
  123.7 3.3 copy-start.36
  123.7 3.9 copy-start.15
  123.7 4.5 copy-start.13
  124.7 5.8 copy-start.38
  124.7 5.9 copy-start.24
  126.8 335.3 %all-reduce.13.cloned.1.call-start = ((), (), s32[]{:S(2)}) async-start(), calls=%async_computation.5 | async-start | bytes 1310720 | tf_op jit(solution)/shard_map/psum | solution.py:93
  131.5 1.5 copy-start.1
  272.0 2.3 copy-start.9
  276.5 1.3 copy-start.4
  281.8 25.1 %copy-start.31 = (f32[64]{0:T(128)S(1)}, f32[64]{0:T(128)}, u32[]{:S(2)}) copy-start(f32[64]{0:T(128)} %get-tuple-element.32) | copy-start | bytes 772
  308.8 6.0 copy-start.25
  308.8 6.0 copy-start.27
  308.8 6.0 copy-start.28
  308.8 6.0 copy-start.29
  308.8 6.6 copy-start.39
  314.5 332.1 %all-reduce.11.cloned.1.call-start = ((), (), s32[]{:S(2)}) async-start(), calls=%async_computation.4 | async-start | bytes 1310720 | tf_op jit(solution)/shard_map/psum | solution.py:93
  323.1 141.2 %copy-start.2 = (f32[80,8,512]{2,1,0:T(8,128)S(1)}, f32[80,8,512]{2,1,0:T(8,128)}, u32[]{:S(2)}) copy-start(f32[80,8,512]{2,1,0:T(8,128)} %copy-done.1) | copy-start | bytes 3932164
  468.2 1.3 copy-start.5
  496.0 3.1 copy-start.37
  496.0 3.2 copy-start.26
  498.1 150.2 %copy-start.17 = (s32[8,1,8]{2,1,0:T(1,128)S(1)}, s32[8,1,8]{2,1,0:T(1,128)}, u32[]{:S(2)}) copy-start(s32[8,1,8]{2,1,0:T(1,128)} %get-tuple-element.75) | copy-start | bytes 772
  499.0 149.8 %copy-start = (f32[80,8,512]{2,0,1:T(8,128)S(1)}, f32[80,8,512]{2,0,1:T(8,128)}, u32[]{:S(2)}) copy-start(f32[80,8,512]{2,0,1:T(8,128)} %get-tuple-element.63) | copy-start | bytes 3932164
  499.1 332.2 %all-reduce.9.cloned.1.call-start = ((), (), s32[]{:S(2)}) async-start(), calls=%async_computation.3 | async-start | bytes 1310720 | tf_op jit(solution)/shard_map/psum | solution.py:93
  650.2 1.3 copy-start.7
  652.8 5.1 copy-start.34
  655.6 23.6 %copy-start.32 = (f32[64]{0:T(128)S(1)}, f32[64]{0:T(128)}, u32[]{:S(2)}) copy-start(f32[64]{0:T(128)} %get-tuple-element.42) | copy-start | bytes 772
  655.6 23.6 %copy-start.33 = (f32[64]{0:T(128)S(1)}, f32[64]{0:T(128)}, u32[]{:S(2)}) copy-start(f32[64]{0:T(128)} %get-tuple-element.43) | copy-start | bytes 772
  655.6 23.7 %copy-start.30 = (f32[64]{0:T(128)S(1)}, f32[64]{0:T(128)}, u32[]{:S(2)}) copy-start(f32[64]{0:T(128)} %get-tuple-element.30) | copy-start | bytes 772
  682.7 150.3 %copy-start.16 = (s32[8,1,8]{2,1,0:T(1,128)S(1)}, s32[8,1,8]{2,1,0:T(1,128)}, u32[]{:S(2)}) copy-start(s32[8,1,8]{2,1,0:T(1,128)} %get-tuple-element.74) | copy-start | bytes 772
  834.9 1.3 copy-start.8
  (1 other events, 1.1 us)
Sparse Core Ops, SparseCore 0:
  126.9 145.1 all-reduce.14
  314.6 147.3 all-reduce.12
  499.2 147.3 all-reduce.10
  683.8 147.4 all-reduce.8
where the time goes:
time: 845 us; the launch traced here: 844 us
  waiting for transfers between devices  601 us (71%)
  blocking collectives  83.8 us (10%)
  local copies, waits for them, and re-layouts  67.1 us (8%)
  other arithmetic  33.7 us (4%)
  starting transfers between devices  26.6 us (3%)
  matrix products  17.7 us (2%)
  between operations  14.1 us (2%)
    psum x4, waiting for transfers between devices, local(): inc_all, scl_all = lax.psum((placed_inc, placed_scl), 'cols')  573 us
    psum x4, blocking collectives, local(): lax.psum(jnp.sum(jnp.where(inside[None], picked, 0.0), axis=2) / pick_cou...  83.8 us
    all_to_all x1, waiting for transfers between devices, local(): lax.all_to_all(state, 'mem', split_axis=1, concat_axis=0, tiled=True)  18.6 us
  transfers between devices with their start and end apart: 7, of which 6 were waited for; matrix products, arithmetic and copies ran while one was open for 4% of the time, Pallas kernels for 0%

commit v1 on v0

--- a/solution.py
+++ b/solution.py
@@ -81,8 +81,11 @@
         inside = (local_cell >= 0) & (local_cell < cell_count) & (obs_pos[batch_no] >= 0)[:, None]
         flat_cells = jnp.clip(local_cell, 0, cell_count - 1).reshape(-1)
         picked = jnp.take(ensemble, flat_cells, axis=1).reshape(members, slot_count, pick_count)
-        prior_obs = lax.psum(
-            jnp.sum(jnp.where(inside[None], picked, 0.0), axis=2) / pick_count, "mem"
+        prior_obs = jnp.sum(
+            lax.all_gather(
+                jnp.sum(jnp.where(inside[None], picked, 0.0), axis=2) / pick_count, "mem"
+            ),
+            axis=0,
         )
         increment, scaled = innovations(
             prior_obs, observed[batch_no], obs_noise[batch_no], obs_flag[batch_no]

time: 845 us -> 809 us (0.957)
  blocking collectives: 83.8 us -> 51 us
    psum x4 -> x0, blocking collectives: 83.8 us -> none  [local(): lax.psum(jnp.sum(jnp.where(inside[None], picked, 0.0), axis=2) / pick_cou...]
    all_gather x0 -> x4, blocking collectives: none -> 51 us  [local(): lax.all_gather(jnp.sum(jnp.where(inside[None], picked, 0.0), axis=2) / pi...]
where the time goes in v1:
time: 809 us; the launch traced here: 808 us
  waiting for transfers between devices  598 us (74%)
  local copies, waits for them, and re-layouts  67.1 us (8%)
  blocking collectives  51 us (6%)
  other arithmetic  33.5 us (4%)
  starting transfers between devices  26.6 us (3%)
  matrix products  17.7 us (2%)
  between operations  14 us (2%)
    psum x4, waiting for transfers between devices, local(): inc_all, scl_all = lax.psum((placed_inc, placed_scl), 'cols')  570 us
    all_gather x4, blocking collectives, local(): lax.all_gather(jnp.sum(jnp.where(inside[None], picked, 0.0), axis=2) / pi...  51 us
    all_to_all x1, waiting for transfers between devices, local(): lax.all_to_all(state, 'mem', split_axis=1, concat_axis=0, tiled=True)  18.6 us
  transfers between devices with their start and end apart: 7, of which 6 were waited for; matrix products, arithmetic and copies ran while one was open for 4% of the time, Pallas kernels for 0%

profile of v1, /device:TPU:2, one launch (start us, length us, event | category | flops | bytes accessed | tf_op | source)
XLA Modules:
  0.0 808.0 jit_solution(6642324293531700160)
XLA Ops:
  10.0 7.9 scatter_fusion.1
  19.1 11.5 %all-to-all-start.2 = ((f32[4,32,2,2]{0,3,2,1:T(2,128)}), f32[4,32,2,2]{0,3,2,1:T(2,128)S(1)}, u32[]{:S(2)}, u32[]{:S(2)}) async-start(f32[4,32,2,2]{0,3,2,1:T(2,128)} %copy.270), calls=%async_computation.2 | async-start | bytes 131072 | tf_op jit(solution)/shard_map/all_to_all | solution.py:66
  31.4 7.9 scatter_fusion
  40.0 1.2 copy.348
  41.3 2.2 copy.253
  43.5 9.8 %all-to-all-start.1 = ((s32[4,32,2,7]{3,2,0,1:T(2,128)}), s32[4,32,2,7]{3,2,0,1:T(2,128)S(1)}, u32[]{:S(2)}, u32[]{:S(2)}) async-start(s32[4,32,2,7]{3,2,0,1:T(2,128)} %copy.261), calls=%async_computation.1 | async-start | bytes 262144 | tf_op jit(solution)/shard_map/all_to_all | solution.py:63
  54.2 9.5 %all-to-all-done.1 = s32[4,32,2,7]{3,2,0,1:T(2,128)S(1)} async-done(((s32[4,32,2,7]{3,2,0,1:T(2,128)}), s32[4,32,2,7]{3,2,0,1:T(2,128)S(1)}, u32[]{:S(2)}, u32[]{:S(2)}) %all-to-all-start.1) | async-done | bytes 7200 | tf_op jit(solution)/shard_map/all_to_all | solution.py:63
  63.7 4.8 all-to-all-start
  75.7 18.6 %all-to-all-done = f32[10,8,4096]{2,0,1:T(8,128)S(1)} async-done(((f32[10,8,4096]{2,0,1:T(8,128)}), f32[10,8,4096]{2,0,1:T(8,128)S(1)}, u32[]{:S(2)}, u32[]{:S(2)}) %all-to-all-start) | async-done | bytes 1310752 | tf_op jit(solution)/shard_map/all_to_all | solution.py:76
  94.5 1.8 copy.266
  96.3 2.4 gather_fusion
  99.8 12.2 %all-gather.4 = f32[8,80,64]{1,2,0:T(8,128)S(1)} all-gather(f32[1,80,64]{1,2,0:T(8,128)S(1)} %multiply_bitcast_fusion.3), channel_id=2, replica_groups=mesh['cols'=32,'mem'=8] {'mem'}, dimensions={0}, use_global_device_ids=true | all-gather | bytes 184320 | tf_op jit(solution)/shard_map/all_gather | solution.py:85
  113.0 1.2 scatter_custom_fusion.3
  122.2 1.3 broadcast_subtract_fusion
  123.5 138.5 %all-reduce.15.cloned.1.call-done = (f32[80,8,128]{2,0,1:T(8,128)}, f32[80,8,128]{2,0,1:T(8,128)}) async-done(((f32[80,8,128]{2,0,1:T(8,128)}, f32[80,8,128]{2,0,1:T(8,128)}), (f32[80,8,128]{2,0,1:T(8,128)}, f32[80,8,128]{2,0,1:T(8,128)})) %all-reduce.15.cloned.1.call-update) | async-done | bytes 655376 | tf_op jit(solution)/shard_map/psum | solution.py:96
  262.1 1.8 fusion.129
  264.4 2.1 fusion
  266.7 1.2 copy-done.4
  267.8 1.2 add.365
  269.0 2.8 copy.284
  271.9 2.4 gather_fusion.1
  275.3 12.8 %all-gather.5 = f32[8,80,64]{1,2,0:T(8,128)S(1)} all-gather(f32[1,80,64]{1,2,0:T(8,128)S(1)} %multiply_bitcast_fusion.2), channel_id=3, replica_groups=mesh['cols'=32,'mem'=8] {'mem'}, dimensions={0}, use_global_device_ids=true | all-gather | bytes 184320 | tf_op jit(solution)/shard_map/all_gather | solution.py:85
  289.1 1.8 scatter_custom_fusion.5
  291.0 2.0 copy.288
  292.9 1.8 scatter_custom_fusion.4
  294.7 2.0 copy.286
  298.9 1.8 copy.278
  300.7 2.7 reshape.689
  303.4 1.9 add_reduce_fusion
  305.4 138.1 %all-reduce.13.cloned.1.call-done = (f32[80,8,128]{2,0,1:T(8,128)}, f32[80,8,128]{2,0,1:T(8,128)}) async-done(((f32[80,8,128]{2,0,1:T(8,128)}, f32[80,8,128]{2,0,1:T(8,128)}), (f32[80,8,128]{2,0,1:T(8,128)}, f32[80,8,128]{2,0,1:T(8,128)})) %all-reduce.13.cloned.1.call-update) | async-done | bytes 655376 | tf_op jit(solution)/shard_map/psum | solution.py:96
  443.4 1.7 fusion.130
  445.7 3.9 fusion.126
  449.7 1.2 copy-done.5
  454.6 12.8 %all-gather.6 = f32[8,80,64]{1,2,0:T(8,128)S(1)} all-gather(f32[1,80,64]{1,2,0:T(8,128)S(1)} %multiply_bitcast_fusion.1), channel_id=4, replica_groups=mesh['cols'=32,'mem'=8] {'mem'}, dimensions={0}, use_global_device_ids=true | all-gather | bytes 184320 | tf_op jit(solution)/shard_map/all_gather | solution.py:85
  468.4 1.2 scatter_custom_fusion.7
  472.8 146.5 %all-reduce.11.cloned.1.call-done = (f32[80,8,128]{2,0,1:T(8,128)}, f32[80,8,128]{2,0,1:T(8,128)}) async-done(((f32[80,8,128]{2,0,1:T(8,128)}, f32[80,8,128]{2,0,1:T(8,128)}), (f32[80,8,128]{2,0,1:T(8,128)}, f32[80,8,128]{2,0,1:T(8,128)})) %all-reduce.11.cloned.1.call-update) | async-done | bytes 655376 | tf_op jit(solution)/shard_map/psum | solution.py:96
  619.4 1.7 fusion.131
  621.6 1.4 fusion.10
  623.1 1.2 copy-done.7
  624.3 1.2 add.390
  625.5 2.8 copy.308
  628.3 2.3 gather_fusion.3
  631.0 13.1 %all-gather.7 = f32[8,80,64]{1,2,0:T(8,128)S(1)} all-gather(f32[1,80,64]{1,2,0:T(8,128)S(1)} %multiply_bitcast_fusion), channel_id=5, replica_groups=mesh['cols'=32,'mem'=8] {'mem'}, dimensions={0}, use_global_device_ids=true | all-gather | bytes 184320 | tf_op jit(solution)/shard_map/all_gather | solution.py:85
  648.6 146.7 %all-reduce.9.cloned.1.call-done = (f32[80,8,128]{2,0,1:T(8,128)}, f32[80,8,128]{2,0,1:T(8,128)}) async-done(((f32[80,8,128]{2,0,1:T(8,128)}, f32[80,8,128]{2,0,1:T(8,128)}), (f32[80,8,128]{2,0,1:T(8,128)}, f32[80,8,128]{2,0,1:T(8,128)})) %all-reduce.9.cloned.1.call-update) | async-done | bytes 655376 | tf_op jit(solution)/shard_map/psum | solution.py:96
  795.4 1.7 fusion.132
  797.6 1.4 convolution_bitcast_fusion
  799.1 1.2 copy-done.8
  800.3 1.2 add.402
  (200 shorter events, 43.3 us)
Async XLA Ops:
  6.5 24.8 %copy-start.10 = (s32[4,32,2,7]{3,2,1,0:T(2,128)S(1)}, s32[4,32,2,7]{3,2,1,0:T(2,128)}, u32[]{:S(2)}) copy-start(s32[4,32,2,7]{3,2,1,0:T(2,128)} %constant.122.clone.1) | copy-start | bytes 21508
  6.5 24.1 %copy-start.18 = (s32[8,4,8]{2,1,0:T(4,128)S(1)}, s32[8,4,8]{2,1,0:T(4,128)}, u32[]{:S(2)}) copy-start(s32[8,4,8]{2,1,0:T(4,128)} %param.21) | copy-start | bytes 3076
  6.5 24.7 %copy-start.40 = (s32[4,32]{1,0:T(4,128)S(1)}, s32[4,32]{1,0:T(4,128)}, u32[]{:S(2)}) copy-start(s32[4,32]{1,0:T(4,128)} %param.20) | copy-start | bytes 1540
  6.5 24.7 %copy-start.21 = (s32[4,32,4]{1,2,0:T(4,128)S(1)}, s32[4,32,4]{1,2,0:T(4,128)}, u32[]{:S(2)}) copy-start(s32[4,32,4]{1,2,0:T(4,128)} %param.19) | copy-start | bytes 6148
  6.5 24.7 %copy-start.41 = (s32[4,32]{1,0:T(4,128)S(1)}, s32[4,32]{1,0:T(4,128)}, u32[]{:S(2)}) copy-start(s32[4,32]{1,0:T(4,128)} %param.18) | copy-start | bytes 1540
  18.0 22.0 %copy-start.11 = (f32[10,32768]{1,0:T(8,128)S(1)}, f32[10,32768]{1,0:T(8,128)}, u32[]{:S(2)}) copy-start(f32[10,32768]{1,0:T(8,128)} %param.14) | copy-start | bytes 3932164
  19.1 24.4 %all-to-all-start.2 = ((f32[4,32,2,2]{0,3,2,1:T(2,128)}), f32[4,32,2,2]{0,3,2,1:T(2,128)S(1)}, u32[]{:S(2)}, u32[]{:S(2)}) async-start(f32[4,32,2,2]{0,3,2,1:T(2,128)} %copy.270), calls=%async_computation.2 | async-start | bytes 131072 | tf_op jit(solution)/shard_map/all_to_all | solution.py:66
  43.5 20.2 %all-to-all-start.1 = ((s32[4,32,2,7]{3,2,0,1:T(2,128)}), s32[4,32,2,7]{3,2,0,1:T(2,128)S(1)}, u32[]{:S(2)}, u32[]{:S(2)}) async-start(s32[4,32,2,7]{3,2,0,1:T(2,128)} %copy.261), calls=%async_computation.1 | async-start | bytes 262144 | tf_op jit(solution)/shard_map/all_to_all | solution.py:63
  63.7 30.5 %all-to-all-start = ((f32[10,8,4096]{2,0,1:T(8,128)}), f32[10,8,4096]{2,0,1:T(8,128)S(1)}, u32[]{:S(2)}, u32[]{:S(2)}) async-start(f32[10,8,4096]{2,0,1:T(8,128)} %copy.253), calls=%async_computation | async-start | bytes 4194304 | tf_op jit(solution)/shard_map/all_to_all | solution.py:76
  68.6 193.5 %all-reduce.15.cloned.1.call-start = ((), (), s32[]{:S(2)}) async-start(), calls=%async_computation.6 | async-start | bytes 1310720 | tf_op jit(solution)/shard_map/psum | solution.py:96
  70.2 24.1 %copy-start.12 = (s32[1,64,4]{2,1,0:T(8,128)}, s32[1,64,4]{2,1,0:T(8,128)S(1)}, u32[]{:S(2)}) copy-start(s32[1,64,4]{2,1,0:T(8,128)S(1)} %get-tuple-element.79) | copy-start | bytes 3076
  70.2 24.1 %copy-start.14 = (s32[1,64,4]{2,1,0:T(8,128)}, s32[1,64,4]{2,1,0:T(8,128)S(1)}, u32[]{:S(2)}) copy-start(s32[1,64,4]{2,1,0:T(8,128)S(1)} %get-tuple-element.76) | copy-start | bytes 3076
  94.5 1.9 copy-start.3
  114.2 3.3 copy-start.19
  114.2 3.3 copy-start.20
  114.2 3.3 copy-start.22
  114.2 3.3 copy-start.23
  114.2 3.3 copy-start.35
  114.2 3.3 copy-start.36
  114.2 3.9 copy-start.15
  114.2 4.5 copy-start.13
  115.2 5.8 copy-start.38
  115.2 5.9 copy-start.24
  117.3 326.2 %all-reduce.13.cloned.1.call-start = ((), (), s32[]{:S(2)}) async-start(), calls=%async_computation.5 | async-start | bytes 1310720 | tf_op jit(solution)/shard_map/psum | solution.py:96
  122.0 1.5 copy-start.1
  262.0 2.3 copy-start.9
  266.5 1.3 copy-start.4
  271.9 17.3 %copy-start.31 = (f32[64]{0:T(128)S(1)}, f32[64]{0:T(128)}, u32[]{:S(2)}) copy-start(f32[64]{0:T(128)} %get-tuple-element.40) | copy-start | bytes 772
  290.9 6.0 copy-start.25
  290.9 6.0 copy-start.27
  291.0 6.0 copy-start.28
  291.0 6.0 copy-start.29
  291.0 6.6 copy-start.39
  296.7 322.7 %all-reduce.11.cloned.1.call-start = ((), (), s32[]{:S(2)}) async-start(), calls=%async_computation.4 | async-start | bytes 1310720 | tf_op jit(solution)/shard_map/psum | solution.py:96
  305.3 140.3 %copy-start.2 = (f32[80,8,512]{2,1,0:T(8,128)S(1)}, f32[80,8,512]{2,1,0:T(8,128)}, u32[]{:S(2)}) copy-start(f32[80,8,512]{2,1,0:T(8,128)} %copy-done.1) | copy-start | bytes 3932164
  449.6 1.3 copy-start.5
  469.6 3.1 copy-start.37
  469.6 3.2 copy-start.26
  471.7 149.4 %copy-start.17 = (s32[8,1,8]{2,1,0:T(1,128)S(1)}, s32[8,1,8]{2,1,0:T(1,128)}, u32[]{:S(2)}) copy-start(s32[8,1,8]{2,1,0:T(1,128)} %get-tuple-element.83) | copy-start | bytes 772
  472.6 149.0 %copy-start = (f32[80,8,512]{2,0,1:T(8,128)S(1)}, f32[80,8,512]{2,0,1:T(8,128)}, u32[]{:S(2)}) copy-start(f32[80,8,512]{2,0,1:T(8,128)} %get-tuple-element.71) | copy-start | bytes 3932164
  472.6 322.7 %all-reduce.9.cloned.1.call-start = ((), (), s32[]{:S(2)}) async-start(), calls=%async_computation.3 | async-start | bytes 1310720 | tf_op jit(solution)/shard_map/psum | solution.py:96
  623.0 1.3 copy-start.7
  625.5 5.1 copy-start.34
  628.3 16.0 %copy-start.32 = (f32[64]{0:T(128)S(1)}, f32[64]{0:T(128)}, u32[]{:S(2)}) copy-start(f32[64]{0:T(128)} %get-tuple-element.50) | copy-start | bytes 772
  628.3 16.1 %copy-start.33 = (f32[64]{0:T(128)S(1)}, f32[64]{0:T(128)}, u32[]{:S(2)}) copy-start(f32[64]{0:T(128)} %get-tuple-element.51) | copy-start | bytes 772
  628.3 16.1 %copy-start.30 = (f32[64]{0:T(128)S(1)}, f32[64]{0:T(128)}, u32[]{:S(2)}) copy-start(f32[64]{0:T(128)} %get-tuple-element.38) | copy-start | bytes 772
  647.6 149.4 %copy-start.16 = (s32[8,1,8]{2,1,0:T(1,128)S(1)}, s32[8,1,8]{2,1,0:T(1,128)}, u32[]{:S(2)}) copy-start(s32[8,1,8]{2,1,0:T(1,128)} %get-tuple-element.82) | copy-start | bytes 772
  799.0 1.3 copy-start.8
  (1 other events, 1.1 us)
Sparse Core Ops, SparseCore 0:
  117.4 144.6 all-reduce.14
  296.8 146.5 all-reduce.12
  472.7 146.5 all-reduce.10
  648.7 146.5 all-reduce.8
